TPU v7x, 32 devices: a whole 2x2x4 slice. The times are simulated.
32 devices in a mesh: dp: 2 (over x), row: 4 (over z), col: 4 (over y, core).
Axes of the slice: x: 2, y: 2, z: 4, core: 2. Of those that a mesh axis runs over, the one named last changes fastest.
Arguments:
- hidden_in: bfloat16 [4096, 1024], P(('dp', 'row'), 'col'), may hold values from -18 to 18
- doc_ids: int32 [8, 512], P(('dp', 'row')), may hold values from 0 to 3, as said below
- w_qkv: bfloat16 [1024, 3, 1024], P('row', None, 'col'), may hold values from -0.1875 to 0.1875
- query_bias: float32 [1024], P('col'), may hold values from -3 to 3
- value_bias: float32 [1024], P('col'), may hold values from -3 to 3
- w_out: bfloat16 [1024, 1024], P('col', 'row'), may hold values from -0.75 to 0.75
- out_bias: float32 [1024], P('col'), may hold values from -3 to 3
- norm_gain: float32 [1024], P('col'), may hold values from 0.5 to 1.5
- norm_shift: float32 [1024], P('col'), may hold values from -3 to 3
- w_up: bfloat16 [1024, 4096], P('row', 'col'), may hold values from -0.1875 to 0.1875
- up_bias: float32 [4096], P('col'), may hold values from -3 to 3
- w_down: bfloat16 [4096, 1024], P('col', 'row'), may hold values from -0.09375 to 0.09375
- down_bias: float32 [1024], P('col'), may hold values from -3 to 3
- final_gain: float32 [1024], P('col'), may hold values from 0.5 to 1.5
- final_shift: float32 [1024], P('col'), may hold values from -3 to 3
- out_grad: bfloat16 [4096, 1024], P(('dp', 'row'), 'col'), may hold values from -6 to 6
Outputs:
- layer_out: bfloat16 [4096, 1024], P(('dp', 'row'), 'col')
- hidden_grad: float32 [4096, 1024], P(('dp', 'row'), 'col')
- wqkv_grad: float32 [1024, 3, 1024], P('row', None, 'col')
- qbias_grad: float32 [1024], P('col')
- vbias_grad: float32 [1024], P('col')
- wout_grad: float32 [1024, 1024], P('col', 'row')
- obias_grad: float32 [1024], P('col')
- ngain_grad: float32 [1024], P('col')
- nshift_grad: float32 [1024], P('col')
- wup_grad: float32 [1024, 4096], P('row', 'col')
- ubias_grad: float32 [4096], P('col')
- wdown_grad: float32 [4096, 1024], P('col', 'row')
- dbias_grad: float32 [1024], P('col')
- fgain_grad: float32 [1024], P('col')
- fshift_grad: float32 [1024], P('col')
Inputs may be any that keep to these rules, and one draw needn't show every extreme that they name: `doc_ids`: along each sequence the ids never fall, start at 0 and end at 3: every sequence packs four documents, each of 51 tokens or more.
All inputs are finite; a program needn't handle non-finite values.
Results may differ from a plain program's by a relative error of at most 0.015.
Values may be sent and summed in bfloat16 or wider, within the bound.
A program may use at most 128 MiB of HBM per device.

v0:
```python
import jax
import jax.numpy as jnp
from jax import lax
from jax.sharding import PartitionSpec as P

D = 1024
HD = 64
EPS = 1e-12
INV_ROOT_TWO = 0.7071067811865476
INV_ROOT_PI = 0.3989422804014327


def gelu_parts(pre_act):
    cdf_val = 0.5 * (1.0 + lax.erf(pre_act * INV_ROOT_TWO))
    density = jnp.exp(-0.5 * pre_act * pre_act) * INV_ROOT_PI
    return (pre_act * cdf_val, cdf_val + pre_act * density)


def normalize(total, gain, shift):
    mean_val = lax.psum(jnp.sum(total, axis=1), "col") / D
    centered = total - mean_val[:, None]
    variance = lax.psum(jnp.sum(centered * centered, axis=1), "col") / D
    inverse = lax.rsqrt(variance + EPS)[:, None]
    normed = centered * inverse
    return (normed * gain + shift, normed, inverse)


def norm_back(upstream, normed, inverse, gain):
    scaled = upstream * gain
    first_sum, second = lax.psum((jnp.sum(scaled, axis=1), jnp.sum(scaled * normed, axis=1)), "col")
    return inverse * (scaled - first_sum[:, None] / D - normed * (second[:, None] / D))


def spread(block):
    return lax.all_gather(block, "col", axis=1, tiled=True)


def spread_grad(block):
    return lax.all_gather(block, "col", axis=1, tiled=True)


def collect(partial_sum):
    return lax.psum_scatter(partial_sum, "col", scatter_dimension=1, tiled=True)


def collect_back(partial_sum):
    return lax.psum_scatter(partial_sum, "col", scatter_dimension=1, tiled=True)


def seq_scores(query, keys, doc_row):
    same_doc = doc_row[:, None] == doc_row[None, :]
    scores = jnp.einsum("qhd,khd->hqk", query, keys, preferred_element_type=jnp.float32) * HD ** (
        -0.5
    )
    return jnp.where(same_doc[None], scores, -jnp.inf)


def attend_seq(inputs_seq):
    query, keys, values, doc_row = inputs_seq
    scores = seq_scores(query, keys, doc_row)
    top_score = jnp.max(scores, axis=-1, keepdims=True)
    log_total = top_score + jnp.log(jnp.sum(jnp.exp(scores - top_score), axis=-1, keepdims=True))
    prob_bf = jnp.exp(scores - log_total).astype(jnp.bfloat16)
    context = jnp.einsum(
        "hqk,khd->qhd", prob_bf, values, preferred_element_type=jnp.float32
    ).astype(jnp.bfloat16)
    return (context, log_total)


def attend_back(inputs_seq):
    query, keys, values, doc_row, ctx_back, log_total = inputs_seq
    prob_f = jnp.exp(seq_scores(query, keys, doc_row) - log_total)
    v_back = jnp.einsum(
        "hqk,qhd->khd", prob_f.astype(jnp.bfloat16), ctx_back, preferred_element_type=jnp.float32
    )
    d_prob = jnp.einsum("qhd,khd->hqk", ctx_back, values, preferred_element_type=jnp.float32)
    row_delta = jnp.sum(prob_f * d_prob, axis=-1, keepdims=True)
    score_back = (prob_f * (d_prob - row_delta) * HD ** (-0.5)).astype(jnp.bfloat16)
    q_back = jnp.einsum("hqk,khd->qhd", score_back, keys, preferred_element_type=jnp.float32)
    k_back = jnp.einsum("hqk,qhd->khd", score_back, query, preferred_element_type=jnp.float32)
    return (q_back, k_back, v_back)


def per_device(
    hidden_in,
    doc_ids,
    w_qkv,
    query_bias,
    value_bias,
    w_out,
    out_bias,
    norm_gain,
    norm_shift,
    w_up,
    up_bias,
    w_down,
    down_bias,
    final_gain,
    final_shift,
    out_grad,
):
    f32 = jnp.float32
    bf16 = jnp.bfloat16
    qkv_full, out_full, up_full, down_full = (
        lax.all_gather(w_qkv, "row", axis=0, tiled=True),
        lax.all_gather(w_out, "row", axis=1, tiled=True),
        lax.all_gather(w_up, "row", axis=0, tiled=True),
        lax.all_gather(w_down, "row", axis=1, tiled=True),
    )
    tokens_dev = hidden_in.shape[0]
    col_width = hidden_in.shape[1]
    head_count = col_width // HD
    seq_count = doc_ids.shape[0]
    seq_len = doc_ids.shape[1]
    head_shape = (seq_count, seq_len, head_count, HD)
    x_full = spread(hidden_in)
    projected = jnp.einsum("td,dkc->tkc", x_full, qkv_full, preferred_element_type=f32)
    query = (projected[:, 0] + query_bias).astype(bf16).reshape(head_shape)
    keys = projected[:, 1].astype(bf16).reshape(head_shape)
    values = (projected[:, 2] + value_bias).astype(bf16).reshape(head_shape)
    context, log_total = lax.map(attend_seq, (query, keys, values, doc_ids))
    ctx_rows = context.reshape(tokens_dev, col_width)
    total_one = (
        hidden_in.astype(f32)
        + collect(jnp.dot(ctx_rows, out_full, preferred_element_type=f32))
        + out_bias
    )
    attn_act, normed_one, inverse_one = normalize(total_one, norm_gain, norm_shift)
    attn_bf = attn_act.astype(bf16)
    attn_full = spread(attn_bf)
    up_pre = jnp.dot(attn_full, up_full, preferred_element_type=f32) + up_bias
    act_f, slope = gelu_parts(up_pre)
    act = act_f.astype(bf16)
    total_two = attn_act + collect(jnp.dot(act, down_full, preferred_element_type=f32)) + down_bias
    final, normed_two, inverse_two = normalize(total_two, final_gain, final_shift)
    layer_out = final.astype(bf16)
    grad_top = out_grad.astype(f32)
    fgain_part = jnp.sum(grad_top * normed_two, axis=0)
    fshift_part = jnp.sum(grad_top, axis=0)
    back_two = norm_back(grad_top, normed_two, inverse_two, final_gain)
    back_two_full = spread_grad(back_two.astype(bf16))
    wdown_part = jnp.dot(act.T, back_two_full, preferred_element_type=f32)
    dbias_part = jnp.sum(back_two, axis=0)
    up_back = jnp.dot(back_two_full, down_full.T, preferred_element_type=f32) * slope
    up_back_bf = up_back.astype(bf16)
    wup_part = jnp.dot(attn_full.T, up_back_bf, preferred_element_type=f32)
    ubias_part = jnp.sum(up_back, axis=0)
    attn_back = back_two + collect_back(jnp.dot(up_back_bf, up_full.T, preferred_element_type=f32))
    ngain_part = jnp.sum(attn_back * normed_one, axis=0)
    nshift_part = jnp.sum(attn_back, axis=0)
    back_one = norm_back(attn_back, normed_one, inverse_one, norm_gain)
    back_one_full = spread_grad(back_one.astype(bf16))
    wout_part = jnp.dot(ctx_rows.T, back_one_full, preferred_element_type=f32)
    obias_part = jnp.sum(back_one, axis=0)
    ctx_back = (
        jnp.dot(back_one_full, out_full.T, preferred_element_type=f32)
        .astype(bf16)
        .reshape(head_shape)
    )
    q_back, k_back, v_back = lax.map(
        attend_back, (query, keys, values, doc_ids, ctx_back, log_total)
    )
    q_back = q_back.reshape(tokens_dev, col_width)
    k_back = k_back.reshape(tokens_dev, col_width)
    v_back = v_back.reshape(tokens_dev, col_width)
    qbias_part = jnp.sum(q_back, axis=0)
    vbias_part = jnp.sum(v_back, axis=0)
    qkv_back = jnp.stack([q_back, k_back, v_back], axis=1).astype(bf16)
    wqkv_part = jnp.einsum("td,tkc->dkc", x_full, qkv_back, preferred_element_type=f32)
    hidden_grad = back_one + collect_back(
        jnp.einsum("tkc,dkc->td", qkv_back, qkv_full, preferred_element_type=f32)
    )
    pieces = (
        lax.psum_scatter(
            wqkv_part.astype(jnp.bfloat16), "row", scatter_dimension=0, tiled=True
        ).astype(jnp.float32),
        lax.psum_scatter(
            wout_part.astype(jnp.bfloat16), "row", scatter_dimension=1, tiled=True
        ).astype(jnp.float32),
        lax.psum_scatter(
            wup_part.astype(jnp.bfloat16), "row", scatter_dimension=0, tiled=True
        ).astype(jnp.float32),
        lax.psum_scatter(
            wdown_part.astype(jnp.bfloat16), "row", scatter_dimension=1, tiled=True
        ).astype(jnp.float32),
    )
    wqkv_grad, wout_grad, wup_grad, wdown_grad = (
        lax.psum(pieces[0].astype(jnp.bfloat16), "dp").astype(jnp.float32),
        lax.psum(pieces[1].astype(jnp.bfloat16), "dp").astype(jnp.float32),
        lax.psum(pieces[2].astype(jnp.bfloat16), "dp").astype(jnp.float32),
        lax.psum(pieces[3].astype(jnp.bfloat16), "dp").astype(jnp.float32),
    )
    small_sums = lax.psum(
        (
            qbias_part,
            vbias_part,
            obias_part,
            ngain_part,
            nshift_part,
            ubias_part,
            dbias_part,
            fgain_part,
            fshift_part,
        ),
        ("dp", "row"),
    )
    return (
        layer_out,
        hidden_grad,
        wqkv_grad,
        small_sums[0],
        small_sums[1],
        wout_grad,
        small_sums[2],
        small_sums[3],
        small_sums[4],
        wup_grad,
        small_sums[5],
        wdown_grad,
        small_sums[6],
        small_sums[7],
        small_sums[8],
    )


def solution(mesh):
    placed = (
        P(("dp", "row"), "col"),
        P(("dp", "row"), None),
        P("row", None, "col"),
        P("col"),
        P("col"),
        P("col", "row"),
        P("col"),
        P("col"),
        P("col"),
        P("row", "col"),
        P("col"),
        P("col", "row"),
        P("col"),
        P("col"),
        P("col"),
        P(("dp", "row"), "col"),
    )
    return jax.shard_map(
        per_device,
        mesh=mesh,
        in_specs=placed,
        out_specs=(
            P(("dp", "row"), "col"),
            P(("dp", "row"), "col"),
            P("row", None, "col"),
            P("col"),
            P("col"),
            P("col", "row"),
            P("col"),
            P("col"),
            P("col"),
            P("row", "col"),
            P("col"),
            P("col", "row"),
            P("col"),
            P("col"),
            P("col"),
        ),
        check_vma=False,
    )
```

profile of v0, /device:TPU:0, one launch (start us, length us, event | category | flops | bytes accessed | tf_op | source)
XLA Modules:
  0.0 611.3 jit_solution(2286843427765584200)
XLA Ops:
  11.5 17.6 %all_gather.26 = bf16[256,1024]{1,0:T(8,128)(2,1)S(1)} all-gather(bf16[256,256]{1,0:T(8,128)(2,1)} %param.21), channel_id=1, replica_groups=mesh['dp'=2,'row'=4,'col'=4] {'row'}, dimensions={1}, use_global_device_ids=true | all-gather | bytes 655360 | tf_op jit(solution)/shard_map/all_gather | solution.py:106
  30.0 38.9 %all-gather.10.cloned.1.call-done = bf16[1024,3,256]{0,2,1:T(8,128)(2,1)} async-done(((bf16[256,3,256]{0,2,1:T(8,128)(2,1)}), bf16[1024,3,256]{0,2,1:T(8,128)(2,1)}) %all-gather.10.cloned.1.call-update) | async-done | bytes 1572880 | tf_op jit(solution)/shard_map/all_gather | solution.py:105
  78.8 28.9 %reduce-scatter.9.cloned.1.call-done = f32[512,256]{1,0:T(8,128)} async-done(((f32[512,1024]{1,0:T(8,128)}), f32[512,256]{1,0:T(8,128)}) %reduce-scatter.9.cloned.1.call-update) | async-done | bytes 524304 | tf_op jit(solution)/shard_map/reduce_scatter | solution.py:43
  108.9 5.8 psum.147
  114.9 5.7 psum.148
  122.1 32.7 %all-gather.14.cloned.1.call-done = bf16[1024,1024]{1,0:T(8,128)(2,1)} async-done(((bf16[256,1024]{1,0:T(8,128)(2,1)}), bf16[1024,1024]{1,0:T(8,128)(2,1)}) %all-gather.14.cloned.1.call-update) | async-done | bytes 2097168 | tf_op jit(solution)/shard_map/all_gather | solution.py:107
  154.8 17.6 %all-gather.12.cloned.1.call-done = bf16[512,1024]{1,0:T(8,128)(2,1)} async-done(((bf16[512,256]{1,0:T(8,128)(2,1)}), bf16[512,1024]{1,0:T(8,128)(2,1)}) %all-gather.12.cloned.1.call-update) | async-done | bytes 1048592 | tf_op jit(solution)/shard_map/all_gather | solution.py:35
  172.4 4.9 multiply_convert_fusion.1
  177.4 42.8 %all-gather.16.cloned.1.call-done = bf16[1024,1024]{1,0:T(8,128)(2,1)} async-done(((bf16[1024,256]{1,0:T(8,128)(2,1)}), bf16[1024,1024]{1,0:T(8,128)(2,1)}) %all-gather.16.cloned.1.call-update) | async-done | bytes 2097168 | tf_op jit(solution)/shard_map/all_gather | solution.py:108
  220.1 4.5 fusion.61
  224.7 29.4 %reduce-scatter.11.cloned.1.call-done = f32[512,256]{1,0:T(8,128)} async-done(((f32[512,1024]{1,0:T(8,128)}), f32[512,256]{1,0:T(8,128)}) %reduce-scatter.11.cloned.1.call-update) | async-done | bytes 524304 | tf_op jit(solution)/shard_map/reduce_scatter | solution.py:43
  255.5 5.8 psum.149
  261.5 5.7 psum.150
  267.6 6.3 %all-reduce.2 = (f32[512]{0:T(512)S(1)}, f32[512]{0:T(512)S(1)}) all-reduce(f32[512]{0:T(512)S(1)} %get-tuple-element.84, f32[512]{0:T(512)S(1)} %get-tuple-element.87), channel_id=1, replica_groups=mesh['dp'=2,'row'=4,'col'=4] {'col'}, use_global_device_ids=true, to_apply=%region_15.16 | all-reduce | flops 1024 | bytes 8192 | tf_op jit(solution)/shard_map/psum | solution.py:30
  276.9 17.4 %all-gather.18.cloned.1.call-done = bf16[512,1024]{1,0:T(8,128)(2,1)} async-done(((bf16[512,256]{1,0:T(8,128)(2,1)}), bf16[512,1024]{1,0:T(8,128)(2,1)}) %all-gather.18.cloned.1.call-update) | async-done | bytes 1048592 | tf_op jit(solution)/shard_map/all_gather | solution.py:39
  294.3 4.6 fusion.59
  302.6 31.3 %reduce-scatter.13.cloned.1.call-done = f32[512,256]{1,0:T(8,128)} async-done(((f32[512,1024]{1,0:T(8,128)}), f32[512,256]{1,0:T(8,128)}) %reduce-scatter.13.cloned.1.call-update) | async-done | bytes 524304 | tf_op jit(solution)/shard_map/reduce_scatter | solution.py:47
  335.3 5.8 all-reduce.1
  342.2 4.3 convolution_convert_fusion
  346.6 3.8 convolution_convert_fusion.1
  350.5 9.3 %all-gather.20.cloned.1.call-done = bf16[512,1024]{1,0:T(8,128)(2,1)} async-done(((bf16[512,256]{1,0:T(8,128)(2,1)}), bf16[512,1024]{1,0:T(8,128)(2,1)}) %all-gather.20.cloned.1.call-update) | async-done | bytes 1048592 | tf_op jit(solution)/shard_map/all_gather | solution.py:39
  362.3 4.1 fusion.55
  370.0 3.9 fusion.41
  373.9 8.8 %fusion.56 = (f32[4,64]{1,0:T(4,128)S(1)}, bf16[512,4,64]{0,2,1:T(8,128)(2,1)S(1)}) fusion(bf16[512,4,64]{0,2,1:T(8,128)(2,1)S(1)} %bitcast.55, f32[4,512,512]{1,2,0:T(8,128)} %fusion.41, f32[4,512]{1,0:T(4,128)S(1)} %log_add_fusion, f32[4,512,512]{1,2,0:T(8,128)} %copy-done, pred[512,512]{0,1:T(8,128)(4,1)S(1)} %broadcast_compare_fusion), kind=kOutput, calls=%fused_computation.90 | convolution fusion | flops 146016512 | bytes 9184256 | tf_op jit(solution)/shard_map/while/body/eval_jaxpr/hqk,khd->qhd/dot_general | solution.py:79
  382.9 7.5 %fusion.22 = bf16[4,64,512]{2,1,0:T(8,128)(2,1)S(1)} fusion(f32[4,512,512]{1,2,0:T(8,128)} %fusion.41, f32[512,4,64]{0,2,1:T(8,128)S(1)} %bitcast.51, f32[4,64]{1,0:T(4,128)S(1)} %add.163, f32[4,512,512]{1,2,0:T(8,128)} %copy-done, f32[4,512]{1,0:T(4,128)S(1)} %log_add_fusion, pred[512,512]{0,1:T(8,128)(4,1)S(1)} %broadcast_compare_fusion), kind=kOutput, calls=%fused_computation.28 | convolution fusion | flops 146147840 | bytes 9446400 | tf_op jit(solution)/shard_map/while/body/eval_jaxpr/hqk,qhd->khd/dot_general | solution.py:80
  392.8 3.7 convolution_bitcast_fusion
  396.6 9.1 %reduce-scatter.23.cloned.1.call-done = bf16[1024,256]{1,0:T(8,128)(2,1)} async-done(((bf16[1024,1024]{1,0:T(8,128)(2,1)}), bf16[1024,256]{1,0:T(8,128)(2,1)}) %reduce-scatter.23.cloned.1.call-update) | async-done | bytes 524304 | tf_op jit(solution)/shard_map/reduce_scatter | solution.py:183
  405.7 45.0 %reduce-scatter.21.cloned.1.call-done = bf16[256,1024]{1,0:T(8,128)(2,1)} async-done(((bf16[1024,1024]{1,0:T(8,128)(2,1)}), bf16[256,1024]{1,0:T(8,128)(2,1)}) %reduce-scatter.21.cloned.1.call-update) | async-done | bytes 524304 | tf_op jit(solution)/shard_map/reduce_scatter | solution.py:180
  450.7 23.9 %reduce-scatter.19.cloned.1.call-done = bf16[256,256]{1,0:T(8,128)(2,1)} async-done(((bf16[256,1024]{1,0:T(8,128)(2,1)}), bf16[256,256]{1,0:T(8,128)(2,1)}) %reduce-scatter.19.cloned.1.call-update) | async-done | bytes 131088 | tf_op jit(solution)/shard_map/reduce_scatter | solution.py:177
  474.7 35.9 %reduce-scatter.17.cloned.1.call-done = bf16[256,3,256]{0,2,1:T(8,128)(2,1)} async-done(((bf16[1024,3,256]{0,2,1:T(8,128)(2,1)}), bf16[256,3,256]{0,2,1:T(8,128)(2,1)}) %reduce-scatter.17.cloned.1.call-update) | async-done | bytes 393232 | tf_op jit(solution)/shard_map/reduce_scatter | solution.py:174
  510.7 35.2 %all-reduce = (f32[256]{0:T(256)}, f32[256]{0:T(256)}, f32[256]{0:T(256)}, f32[256]{0:T(256)}, f32[256]{0:T(256)}, /*index=5*/f32[1024]{0:T(1024)}, f32[256]{0:T(256)}, f32[256]{0:T(256)}, f32[256]{0:T(256)}) all-reduce(f32[256]{0:T(256)S(1)} %reduce_sum.188, ...), channel_id=1, replica_groups=mesh['dp'=2,'row'=4,'col'=4] {'dp','row'}, use_global_device_ids=true, to_apply=%region_26.27 | all-reduce | flops 3072 | bytes 24576 | tf_op jit(solution)/shard_map/psum | solution.py:193
  547.9 49.0 %all-reduce.6.cloned.1.call-done = (bf16[256,3,256]{0,2,1:T(8,128)(2,1)}, bf16[256,256]{1,0:T(8,128)(2,1)}, bf16[256,1024]{1,0:T(8,128)(2,1)}, bf16[1024,256]{1,0:T(8,128)(2,1)}) async-done(((bf16[256,3,256]{0,2,1:T(8,128)(2,1)}, bf16[256,256]{1,0:T(8,128)(2,1)}, bf16[256,1024]{1,0:T(8,128)(2,1)}, bf16[1024,256]{1,0:T(8,128)(2,1)}), (bf16[256,3,256]{0,2,1:T(8,128)(2,1)}, bf16[256,256]{1,0:T(8,128)(2,1)}, ...) | async-done | bytes 1572880 | tf_op jit(solution)/shard_map/psum | solution.py:188
  (116 shorter events, 47.9 us)
Async XLA Ops:
  7.2 22.9 %all-gather.8.cloned.1.call-start = ((), (), s32[]{:S(2)}) async-start(), calls=%async_computation.8 | async-start | bytes 1310720 | tf_op jit(solution)/shard_map/all_gather | solution.py:35
  7.9 61.1 %all-gather.10.cloned.1.call-start = ((), (), s32[]{:S(2)}) async-start(), calls=%async_computation.9 | async-start | bytes 1966080 | tf_op jit(solution)/shard_map/all_gather | solution.py:105
  9.9 97.8 %reduce-scatter.9.cloned.1.call-start = ((), (), s32[]{:S(2)}) async-start(), calls=%async_computation.10 | async-start | bytes 2621440 | tf_op jit(solution)/shard_map/reduce_scatter | solution.py:43
  73.4 2.2 copy-start
  75.6 32.1 %copy-start.4 = (bf16[512,256]{1,0:T(8,128)(2,1)S(1)}, bf16[512,256]{1,0:T(8,128)(2,1)}, u32[]{:S(2)}) copy-start(bf16[512,256]{1,0:T(8,128)(2,1)} %param.16) | copy-start | bytes 786436
  75.6 32.1 %copy-start.11 = (f32[256]{0:T(256)S(1)}, f32[256]{0:T(256)}, u32[]{:S(2)}) copy-start(f32[256]{0:T(256)} %param.22) | copy-start | bytes 3076
  75.6 44.9 %copy-start.8 = (f32[256]{0:T(256)S(1)}, f32[256]{0:T(256)}, u32[]{:S(2)}) copy-start(f32[256]{0:T(256)} %param.23) | copy-start | bytes 3076
  75.7 44.9 %copy-start.9 = (f32[256]{0:T(256)S(1)}, f32[256]{0:T(256)}, u32[]{:S(2)}) copy-start(f32[256]{0:T(256)} %param.24) | copy-start | bytes 3076
  76.3 96.1 %copy-start.17 = (f32[1024]{0:T(1024)S(1)}, f32[1024]{0:T(1024)}, u32[]{:S(2)}) copy-start(f32[1024]{0:T(1024)} %param.26) | copy-start | bytes 12292
  78.1 76.7 %all-gather.14.cloned.1.call-start = ((), (), s32[]{:S(2)}) async-start(), calls=%async_computation.12 | async-start | bytes 2621440 | tf_op jit(solution)/shard_map/all_gather | solution.py:107
  78.7 93.7 %all-gather.12.cloned.1.call-start = ((), (), s32[]{:S(2)}) async-start(), calls=%async_computation.11 | async-start | bytes 1310720 | tf_op jit(solution)/shard_map/all_gather | solution.py:35
  121.5 98.6 %all-gather.16.cloned.1.call-start = ((), (), s32[]{:S(2)}) async-start(), calls=%async_computation.13 | async-start | bytes 2621440 | tf_op jit(solution)/shard_map/all_gather | solution.py:108
  122.1 132.1 %reduce-scatter.11.cloned.1.call-start = ((), (), s32[]{:S(2)}) async-start(), calls=%async_computation.14 | async-start | bytes 2621440 | tf_op jit(solution)/shard_map/reduce_scatter | solution.py:43
  220.1 34.0 %copy-start.12 = (f32[256]{0:T(256)S(1)}, f32[256]{0:T(256)}, u32[]{:S(2)}) copy-start(f32[256]{0:T(256)} %param.28) | copy-start | bytes 3076
  220.1 47.0 %copy-start.5 = (bf16[512,256]{1,0:T(8,128)(2,1)S(1)}, bf16[512,256]{1,0:T(8,128)(2,1)}, u32[]{:S(2)}) copy-start(bf16[512,256]{1,0:T(8,128)(2,1)} %param.31) | copy-start | bytes 786436
  220.1 47.0 %copy-start.10 = (f32[256]{0:T(256)S(1)}, f32[256]{0:T(256)}, u32[]{:S(2)}) copy-start(f32[256]{0:T(256)} %param.29) | copy-start | bytes 3076
  224.6 49.3 %copy-start.13 = (f32[256]{0:T(256)S(1)}, f32[256]{0:T(256)}, u32[]{:S(2)}) copy-start(f32[256]{0:T(256)} %param.30) | copy-start | bytes 3076
  224.7 69.7 %all-gather.18.cloned.1.call-start = ((), (), s32[]{:S(2)}) async-start(), calls=%async_computation.15 | async-start | bytes 1310720 | tf_op jit(solution)/shard_map/all_gather | solution.py:39
  276.6 57.2 %reduce-scatter.13.cloned.1.call-start = ((), (), s32[]{:S(2)}) async-start(), calls=%async_computation.16 | async-start | bytes 2621440 | tf_op jit(solution)/shard_map/reduce_scatter | solution.py:47
  294.3 5.6 copy-start.14
  298.9 1.0 copy-start.18
  302.5 57.2 %all-gather.20.cloned.1.call-start = ((), (), s32[]{:S(2)}) async-start(), calls=%async_computation.17 | async-start | bytes 1310720 | tf_op jit(solution)/shard_map/all_gather | solution.py:39
  342.2 4.4 copy-start.16
  342.2 63.6 %reduce-scatter.23.cloned.1.call-start = ((), (), s32[]{:S(2)}) async-start(), calls=%async_computation.22 | async-start | bytes 2621440 | tf_op jit(solution)/shard_map/reduce_scatter | solution.py:183
  346.5 104.2 %reduce-scatter.21.cloned.1.call-start = ((), (), s32[]{:S(2)}) async-start(), calls=%async_computation.21 | async-start | bytes 2621440 | tf_op jit(solution)/shard_map/reduce_scatter | solution.py:180
  350.4 124.2 %reduce-scatter.19.cloned.1.call-start = ((), (), s32[]{:S(2)}) async-start(), calls=%async_computation.20 | async-start | bytes 655360 | tf_op jit(solution)/shard_map/reduce_scatter | solution.py:177
  359.8 7.7 %copy-start.1 = (bf16[512,1024]{1,0:T(8,128)(2,1)S(1)}, bf16[512,1024]{1,0:T(8,128)(2,1)}, u32[]{:S(2)}) copy-start(bf16[512,1024]{1,0:T(8,128)(2,1)} %all-gather.20.cloned.1.call-done) | copy-start | bytes 3145732
  366.4 7.5 %copy-start.3 = (bf16[512,1,256]{0,2,1:T(8,128)(2,1)S(1)}, bf16[512,1,256]{0,2,1:T(8,128)(2,1)}, u32[]{:S(2)}) copy-start(bf16[512,1,256]{0,2,1:T(8,128)(2,1)} %copy-done.2) | copy-start | bytes 786436
  369.8 140.8 %reduce-scatter.17.cloned.1.call-start = ((), (), s32[]{:S(2)}) async-start(), calls=%async_computation.19 | async-start | bytes 1966080 | tf_op jit(solution)/shard_map/reduce_scatter | solution.py:174
  382.9 7.7 %copy-start.15 = (bf16[512,1024]{1,0:T(8,128)(2,1)S(1)}, bf16[512,1024]{1,0:T(8,128)(2,1)}, u32[]{:S(2)}) copy-start(bf16[512,1024]{1,0:T(8,128)(2,1)} %all-gather.8.cloned.1.call-done) | copy-start | bytes 3145732
  392.8 153.2 %reduce-scatter.15.cloned.1.call-start = ((), (), s32[]{:S(2)}) async-start(), calls=%async_computation.18 | async-start | bytes 2621440 | tf_op jit(solution)/shard_map/reduce_scatter | solution.py:47
  396.6 200.3 %all-reduce.6.cloned.1.call-start = ((), (), s32[]{:S(2)}) async-start(), calls=%async_computation.23 | async-start | bytes 3145728 | tf_op jit(solution)/shard_map/psum | solution.py:188
  (3 other events, 2.1 us)
Sparse Core Ops, SparseCore 0:
  9.5 19.5 all-gather.7
  31.2 37.6 all-gather.9
  78.3 29.3 reduce-scatter.8
  109.1 45.6 all-gather.13
  156.8 15.6 all-gather.11
  173.8 46.2 all-gather.15
  224.8 29.3 reduce-scatter.10
  276.8 17.5 all-gather.17
  302.6 31.1 reduce-scatter.12
  342.3 17.4 all-gather.19
  362.1 43.6 reduce-scatter.22
  407.9 42.8 reduce-scatter.20
  453.6 21.0 reduce-scatter.18
  476.8 33.6 reduce-scatter.16
  512.9 29.9 reduce-scatter.14
  545.3 51.5 all-reduce.5
where the time goes:
time: 612 us; the launch traced here: 611 us
  waiting for transfers between devices  413 us (67%)
  blocking collectives  87.8 us (14%)
  matrix products  65.8 us (11%)
  other arithmetic  19.2 us (3%)
  between operations  14.2 us (2%)
  local copies, waits for them, and re-layouts  10.1 us (2%)
    reduce_scatter x2, waiting for transfers between devices, collect(): return lax.psum_scatter(partial_sum, 'col', scatter_dimension=1, tiled=True)  58.4 us
    psum x1, waiting for transfers between devices, per_device(): lax.psum(pieces[0].astype(jnp.bfloat16), 'dp').astype(jnp.float32)  49 us
    reduce_scatter x1, waiting for transfers between devices, per_device(): lax.psum_scatter(wup_part.astype(jnp.bfloat16), 'row', scatter_dimension=...  45 us
    all_gather x1, waiting for transfers between devices, per_device(): lax.all_gather(w_down, 'row', axis=1, tiled=True)  42.8 us
    all_gather x1, waiting for transfers between devices, per_device(): lax.all_gather(w_qkv, 'row', axis=0, tiled=True)  38.9 us
    reduce_scatter x1, waiting for transfers between devices, per_device(): lax.psum_scatter(wqkv_part.astype(jnp.bfloat16), 'row', scatter_dimension...  35.9 us
    psum x1, blocking collectives, per_device(): lax.psum((qbias_part, vbias_part, obias_part, ngain_part, nshift_part, ub...  35.2 us
    all_gather x1, waiting for transfers between devices, per_device(): lax.all_gather(w_up, 'row', axis=0, tiled=True)  32.7 us
  transfers between devices with their start and end apart: 16, of which 14 were waited for; matrix products, arithmetic and copies ran while one was open for 9% of the time, Pallas kernels for 0%

commit v1 on v0

--- a/solution.py
+++ b/solution.py
@@ -8,6 +8,27 @@
 EPS = 1e-12
 INV_ROOT_TWO = 0.7071067811865476
 INV_ROOT_PI = 0.3989422804014327
+
+
+def ring_gather(x, axis, dim):
+    size, place, rows = (lax.axis_size(axis), lax.axis_index(axis), x.shape[dim])
+    ahead = [(i, (i + 1) % size) for i in range(size)]
+    left = [(i, (i - 1) % size) for i in range(size)]
+    whole = jnp.zeros((*x.shape[:dim], size * rows, *x.shape[dim + 1 :]), x.dtype)
+    whole = lax.dynamic_update_slice_in_dim(whole, x, place * rows, axis=dim)
+    from_left = from_right = x
+    middle = size // 2
+    for step in range(1, middle + 1):
+        from_left = lax.ppermute(from_left, axis, ahead)
+        whole = lax.dynamic_update_slice_in_dim(
+            whole, from_left, (place - step) % size * rows, axis=dim
+        )
+        if step < size - middle:
+            from_right = lax.ppermute(from_right, axis, left)
+            whole = lax.dynamic_update_slice_in_dim(
+                whole, from_right, (place + step) % size * rows, axis=dim
+            )
+    return whole
 
 
 def gelu_parts(pre_act):
@@ -104,7 +125,7 @@
     qkv_full, out_full, up_full, down_full = (
         lax.all_gather(w_qkv, "row", axis=0, tiled=True),
         lax.all_gather(w_out, "row", axis=1, tiled=True),
-        lax.all_gather(w_up, "row", axis=0, tiled=True),
+        ring_gather(w_up, "row", 0),
         lax.all_gather(w_down, "row", axis=1, tiled=True),
     )
     tokens_dev = hidden_in.shape[0]

time: 612 us -> 587 us (0.959)
  waiting for transfers between devices: 413 us -> 377 us
  local copies, waits for them, and re-layouts: 10.1 us -> 18.1 us
    ppermute x0 -> x3, waiting for transfers between devices: none -> 36.3 us  [the longest x2 30.4 us: ring_gather(): from_left = lax.ppermute(from_left, axis, ahead)]
    all_gather x1 -> x0, waiting for transfers between devices: 32.7 us -> none  [per_device(): lax.all_gather(w_up, 'row', axis=0, tiled=True)]
    all_gather x1, waiting for transfers between devices: 42.8 us -> 19.1 us  [per_device(): lax.all_gather(w_down, 'row', axis=1, tiled=True)]
    all_gather x2, waiting for transfers between devices: 17.7 us -> 0.02 us  [spread(): return lax.all_gather(block, 'col', axis=1, tiled=True)]
    dynamic_update_slice x0 -> x4, local copies, waits for them, and re-layouts: none -> 6.57 us  [the longest x2 3.73 us: ring_gather(): lax.dynamic_update_slice_in_dim(whole, from_left, (place - step) % size *...]
  transfers between devices with their start and end apart: 16 -> 18, of which waited for: 14 -> 15; matrix products, arithmetic and copies ran while one was open for 9% -> 11% of each run, Pallas kernels for 0% -> 0%
where the time goes in v1:
time: 587 us; the launch traced here: 586 us
  waiting for transfers between devices  377 us (64%)
  blocking collectives  87.7 us (15%)
  matrix products  66 us (11%)
  local copies, waits for them, and re-layouts  18.1 us (3%)
  other arithmetic  17.4 us (3%)
  between operations  14.2 us (2%)
    reduce_scatter x2, waiting for transfers between devices, collect(): return lax.psum_scatter(partial_sum, 'col', scatter_dimension=1, tiled=True)  59.5 us
    psum x1, waiting for transfers between devices, per_device(): lax.psum(pieces[0].astype(jnp.bfloat16), 'dp').astype(jnp.float32)  49 us
    reduce_scatter x1, waiting for transfers between devices, per_device(): lax.psum_scatter(wup_part.astype(jnp.bfloat16), 'row', scatter_dimension=...  45.2 us
    all_gather x1, waiting for transfers between devices, per_device(): lax.all_gather(w_qkv, 'row', axis=0, tiled=True)  39.7 us
    reduce_scatter x1, waiting for transfers between devices, per_device(): lax.psum_scatter(wqkv_part.astype(jnp.bfloat16), 'row', scatter_dimension...  36 us
    psum x1, blocking collectives, per_device(): lax.psum((qbias_part, vbias_part, obias_part, ngain_part, nshift_part, ub...  35.2 us
    reduce_scatter x2, waiting for transfers between devices, collect_back(): return lax.psum_scatter(partial_sum, 'col', scatter_dimension=1, tiled=True)  31.3 us
    ppermute x2, waiting for transfers between devices, ring_gather(): from_left = lax.ppermute(from_left, axis, ahead)  30.4 us
  transfers between devices with their start and end apart: 18, of which 15 were waited for; matrix products, arithmetic and copies ran while one was open for 11% of the time, Pallas kernels for 0%

profile of v1, /device:TPU:0, one launch (start us, length us, event | category | flops | bytes accessed | tf_op | source)
XLA Modules:
  0.0 585.8 jit_solution(3017682937167523054)
XLA Ops:
  11.5 17.6 %all_gather.23 = bf16[256,1024]{1,0:T(8,128)(2,1)S(1)} all-gather(bf16[256,256]{1,0:T(8,128)(2,1)} %param.21), channel_id=1, replica_groups=mesh['dp'=2,'row'=4,'col'=4] {'row'}, dimensions={1}, use_global_device_ids=true | all-gather | bytes 655360 | tf_op jit(solution)/shard_map/all_gather | solution.py:127
  29.3 39.7 %all-gather.9.cloned.1.call-done = bf16[1024,3,256]{0,2,1:T(8,128)(2,1)} async-done(((bf16[256,3,256]{0,2,1:T(8,128)(2,1)}), bf16[1024,3,256]{0,2,1:T(8,128)(2,1)}) %all-gather.9.cloned.1.call-update) | async-done | bytes 1572880 | tf_op jit(solution)/shard_map/all_gather | solution.py:126
  77.9 29.5 %reduce-scatter.9.cloned.1.call-done = f32[512,256]{1,0:T(8,128)} async-done(((f32[512,1024]{1,0:T(8,128)}), f32[512,256]{1,0:T(8,128)}) %reduce-scatter.9.cloned.1.call-update) | async-done | bytes 524304 | tf_op jit(solution)/shard_map/reduce_scatter | solution.py:64
  108.6 5.8 psum.147
  114.6 5.7 psum.148
  125.7 12.9 %collective-permute-done = bf16[256,1024]{1,0:T(8,128)(2,1)} collective-permute-done((bf16[256,1024]{1,0:T(8,128)(2,1)S(1)}, bf16[256,1024]{1,0:T(8,128)(2,1)}, u32[]{:S(2)}, u32[]{:S(2)}) %collective-permute-start) | collective-permute-done | bytes 524320 | tf_op jit(solution)/shard_map/ppermute | solution.py:22
  143.1 5.9 %collective-permute-done.1 = bf16[256,1024]{1,0:T(8,128)(2,1)} collective-permute-done((bf16[256,1024]{1,0:T(8,128)(2,1)S(1)}, bf16[256,1024]{1,0:T(8,128)(2,1)}, u32[]{:S(2)}, u32[]{:S(2)}) %collective-permute-start.1) | collective-permute-done | bytes 524320 | tf_op jit(solution)/shard_map/ppermute | solution.py:27
  150.9 17.5 %collective-permute-done.2 = bf16[256,1024]{1,0:T(8,128)(2,1)} collective-permute-done((bf16[256,1024]{1,0:T(8,128)(2,1)}, bf16[256,1024]{1,0:T(8,128)(2,1)}, u32[]{:S(2)}, u32[]{:S(2)}) %collective-permute-start.2) | collective-permute-done | bytes 524320 | tf_op jit(solution)/shard_map/ppermute | solution.py:22
  170.3 4.6 multiply_convert_fusion.1
  174.9 19.1 %all-gather.13.cloned.1.call-done = bf16[1024,1024]{1,0:T(8,128)(2,1)} async-done(((bf16[1024,256]{1,0:T(8,128)(2,1)}), bf16[1024,1024]{1,0:T(8,128)(2,1)}) %all-gather.13.cloned.1.call-update) | async-done | bytes 2097168 | tf_op jit(solution)/shard_map/all_gather | solution.py:129
  194.0 4.1 fusion.62
  198.2 30.0 %reduce-scatter.11.cloned.1.call-done = f32[512,256]{1,0:T(8,128)} async-done(((f32[512,1024]{1,0:T(8,128)}), f32[512,256]{1,0:T(8,128)}) %reduce-scatter.11.cloned.1.call-update) | async-done | bytes 524304 | tf_op jit(solution)/shard_map/reduce_scatter | solution.py:64
  229.6 5.8 psum.149
  235.6 5.7 psum.150
  241.6 6.3 %all-reduce.2 = (f32[512]{0:T(512)S(1)}, f32[512]{0:T(512)S(1)}) all-reduce(f32[512]{0:T(512)S(1)} %get-tuple-element.84, f32[512]{0:T(512)S(1)} %get-tuple-element.87), channel_id=1, replica_groups=mesh['dp'=2,'row'=4,'col'=4] {'col'}, use_global_device_ids=true, to_apply=%region_15.16 | all-reduce | flops 1024 | bytes 8192 | tf_op jit(solution)/shard_map/psum | solution.py:51
  250.9 17.5 %all-gather.15.cloned.1.call-done = bf16[512,1024]{1,0:T(8,128)(2,1)} async-done(((bf16[512,256]{1,0:T(8,128)(2,1)}), bf16[512,1024]{1,0:T(8,128)(2,1)}) %all-gather.15.cloned.1.call-update) | async-done | bytes 1048592 | tf_op jit(solution)/shard_map/all_gather | solution.py:60
  268.4 4.4 fusion.51
  273.8 4.3 fusion.38
  278.1 31.3 %reduce-scatter.13.cloned.1.call-done = f32[512,256]{1,0:T(8,128)} async-done(((f32[512,1024]{1,0:T(8,128)}), f32[512,256]{1,0:T(8,128)}) %reduce-scatter.13.cloned.1.call-update) | async-done | bytes 524304 | tf_op jit(solution)/shard_map/reduce_scatter | solution.py:68
  310.8 5.8 all-reduce.1
  317.8 4.2 convolution_convert_fusion
  322.1 4.1 convolution_convert_fusion.1
  326.3 9.0 %all-gather.17.cloned.1.call-done = bf16[512,1024]{1,0:T(8,128)(2,1)} async-done(((bf16[512,256]{1,0:T(8,128)(2,1)}), bf16[512,1024]{1,0:T(8,128)(2,1)}) %all-gather.17.cloned.1.call-update) | async-done | bytes 1048592 | tf_op jit(solution)/shard_map/all_gather | solution.py:60
  337.0 4.2 fusion.57
  347.5 8.8 %fusion.58 = (f32[4,64]{1,0:T(4,128)S(1)}, bf16[512,4,64]{0,2,1:T(8,128)(2,1)S(1)}) fusion(bf16[512,4,64]{0,2,1:T(8,128)(2,1)S(1)} %bitcast.55, f32[4,512,512]{1,2,0:T(8,128)} %fusion.41, f32[4,512]{1,0:T(4,128)S(1)} %log_add_fusion, f32[4,512,512]{1,2,0:T(8,128)} %copy-done, pred[512,512]{0,1:T(8,128)(4,1)S(1)} %broadcast_compare_fusion), kind=kOutput, calls=%fused_computation.95 | convolution fusion | flops 146016512 | bytes 9184256 | tf_op jit(solution)/shard_map/while/body/eval_jaxpr/hqk,khd->qhd/dot_general | solution.py:100
  356.4 7.5 %fusion.22 = bf16[4,64,512]{2,1,0:T(8,128)(2,1)S(1)} fusion(f32[4,512,512]{1,2,0:T(8,128)} %fusion.41, f32[512,4,64]{0,2,1:T(8,128)S(1)} %bitcast.51, f32[4,64]{1,0:T(4,128)S(1)} %add.190, f32[4,512,512]{1,2,0:T(8,128)} %copy-done, f32[4,512]{1,0:T(4,128)S(1)} %log_add_fusion, pred[512,512]{0,1:T(8,128)(4,1)S(1)} %broadcast_compare_fusion), kind=kOutput, calls=%fused_computation.28 | convolution fusion | flops 146147840 | bytes 9446400 | tf_op jit(solution)/shard_map/while/body/eval_jaxpr/hqk,qhd->khd/dot_general | solution.py:101
  371.4 9.7 %reduce-scatter.23.cloned.1.call-done = bf16[1024,256]{1,0:T(8,128)(2,1)} async-done(((bf16[1024,1024]{1,0:T(8,128)(2,1)}), bf16[1024,256]{1,0:T(8,128)(2,1)}) %reduce-scatter.23.cloned.1.call-update) | async-done | bytes 524304 | tf_op jit(solution)/shard_map/reduce_scatter | solution.py:204
  381.1 45.2 %reduce-scatter.21.cloned.1.call-done = bf16[256,1024]{1,0:T(8,128)(2,1)} async-done(((bf16[1024,1024]{1,0:T(8,128)(2,1)}), bf16[256,1024]{1,0:T(8,128)(2,1)}) %reduce-scatter.21.cloned.1.call-update) | async-done | bytes 524304 | tf_op jit(solution)/shard_map/reduce_scatter | solution.py:201
  426.3 23.8 %reduce-scatter.19.cloned.1.call-done = bf16[256,256]{1,0:T(8,128)(2,1)} async-done(((bf16[256,1024]{1,0:T(8,128)(2,1)}), bf16[256,256]{1,0:T(8,128)(2,1)}) %reduce-scatter.19.cloned.1.call-update) | async-done | bytes 131088 | tf_op jit(solution)/shard_map/reduce_scatter | solution.py:198
  450.0 36.0 %reduce-scatter.17.cloned.1.call-done = bf16[256,3,256]{0,2,1:T(8,128)(2,1)} async-done(((bf16[1024,3,256]{0,2,1:T(8,128)(2,1)}), bf16[256,3,256]{0,2,1:T(8,128)(2,1)}) %reduce-scatter.17.cloned.1.call-update) | async-done | bytes 393232 | tf_op jit(solution)/shard_map/reduce_scatter | solution.py:195
  486.3 35.2 %all-reduce = (f32[256]{0:T(256)}, f32[256]{0:T(256)}, f32[256]{0:T(256)}, f32[256]{0:T(256)}, f32[256]{0:T(256)}, /*index=5*/f32[1024]{0:T(1024)}, f32[256]{0:T(256)}, f32[256]{0:T(256)}, f32[256]{0:T(256)}) all-reduce(f32[256]{0:T(256)S(1)} %reduce_sum.188, ...), channel_id=1, replica_groups=mesh['dp'=2,'row'=4,'col'=4] {'dp','row'}, use_global_device_ids=true, to_apply=%region_26.27 | all-reduce | flops 3072 | bytes 24576 | tf_op jit(solution)/shard_map/psum | solution.py:214
  523.4 49.0 %all-reduce.6.cloned.1.call-done = (bf16[256,3,256]{0,2,1:T(8,128)(2,1)}, bf16[256,256]{1,0:T(8,128)(2,1)}, bf16[256,1024]{1,0:T(8,128)(2,1)}, bf16[1024,256]{1,0:T(8,128)(2,1)}) async-done(((bf16[256,3,256]{0,2,1:T(8,128)(2,1)}, bf16[256,256]{1,0:T(8,128)(2,1)}, bf16[256,1024]{1,0:T(8,128)(2,1)}, bf16[1024,256]{1,0:T(8,128)(2,1)}), (bf16[256,3,256]{0,2,1:T(8,128)(2,1)}, bf16[256,256]{1,0:T(8,128)(2,1)}, ...) | async-done | bytes 1572880 | tf_op jit(solution)/shard_map/psum | solution.py:209
  (128 shorter events, 61.6 us)
Async XLA Ops:
  7.2 21.9 %copy-start.12 = (s32[1,512]{1,0:T(1,128)S(1)}, s32[1,512]{1,0:T(1,128)}, u32[]{:S(2)}) copy-start(s32[1,512]{1,0:T(1,128)} %param.17) | copy-start | bytes 6148
  7.2 22.1 %all-gather.7.cloned.1.call-start = ((), (), s32[]{:S(2)}) async-start(), calls=%async_computation.8 | async-start | bytes 1310720 | tf_op jit(solution)/shard_map/all_gather | solution.py:56
  7.9 61.1 %all-gather.9.cloned.1.call-start = ((), (), s32[]{:S(2)}) async-start(), calls=%async_computation.9 | async-start | bytes 1966080 | tf_op jit(solution)/shard_map/all_gather | solution.py:126
  9.9 97.5 %reduce-scatter.9.cloned.1.call-start = ((), (), s32[]{:S(2)}) async-start(), calls=%async_computation.10 | async-start | bytes 2621440 | tf_op jit(solution)/shard_map/reduce_scatter | solution.py:64
  76.0 31.4 %copy-start.4 = (bf16[512,256]{1,0:T(8,128)(2,1)S(1)}, bf16[512,256]{1,0:T(8,128)(2,1)}, u32[]{:S(2)}) copy-start(bf16[512,256]{1,0:T(8,128)(2,1)} %param.16) | copy-start | bytes 786436
  76.0 31.4 %copy-start.15 = (f32[256]{0:T(256)S(1)}, f32[256]{0:T(256)}, u32[]{:S(2)}) copy-start(f32[256]{0:T(256)} %param.22) | copy-start | bytes 3076
  77.8 42.4 %copy-start.11 = (f32[256]{0:T(256)S(1)}, f32[256]{0:T(256)}, u32[]{:S(2)}) copy-start(f32[256]{0:T(256)} %param.23) | copy-start | bytes 3076
  77.8 42.4 %copy-start.13 = (f32[256]{0:T(256)S(1)}, f32[256]{0:T(256)}, u32[]{:S(2)}) copy-start(f32[256]{0:T(256)} %param.24) | copy-start | bytes 3076
  77.9 44.0 %copy-start.9 = (bf16[256,1024]{1,0:T(8,128)(2,1)S(1)}, bf16[256,1024]{1,0:T(8,128)(2,1)}, u32[]{:S(2)}) copy-start(bf16[256,1024]{1,0:T(8,128)(2,1)} %param.25) | copy-start | bytes 1572868
  77.9 92.4 %all-gather.11.cloned.1.call-start = ((), (), s32[]{:S(2)}) async-start(), calls=%async_computation.11 | async-start | bytes 1310720 | tf_op jit(solution)/shard_map/all_gather | solution.py:56
  121.2 72.8 %all-gather.13.cloned.1.call-start = ((), (), s32[]{:S(2)}) async-start(), calls=%async_computation.12 | async-start | bytes 2621440 | tf_op jit(solution)/shard_map/all_gather | solution.py:129
  121.8 106.4 %reduce-scatter.11.cloned.1.call-start = ((), (), s32[]{:S(2)}) async-start(), calls=%async_computation.13 | async-start | bytes 2621440 | tf_op jit(solution)/shard_map/reduce_scatter | solution.py:64
  121.9 16.8 %collective-permute-start = (bf16[256,1024]{1,0:T(8,128)(2,1)S(1)}, bf16[256,1024]{1,0:T(8,128)(2,1)}, u32[]{:S(2)}, u32[]{:S(2)}) collective-permute-start(bf16[256,1024]{1,0:T(8,128)(2,1)S(1)} %copy-done.9), channel_id=1, source_target_pairs={{0,4},{4,8},{8,12},{12,0},{1,5},{5,9},{9,13},{13,1},{2,6},{6,10},{... | collective-permute-start | bytes 1572872 | tf_op jit(solution)/shard_map/ppermute | solution.py:22
  123.6 25.4 %collective-permute-start.1 = (bf16[256,1024]{1,0:T(8,128)(2,1)S(1)}, bf16[256,1024]{1,0:T(8,128)(2,1)}, u32[]{:S(2)}, u32[]{:S(2)}) collective-permute-start(bf16[256,1024]{1,0:T(8,128)(2,1)S(1)} %copy-done.9), channel_id=1, source_target_pairs={{0,12},{4,0},{8,4},{12,8},{1,13},{5,1},{9,5},{13,9},{2,14},{6,2},{... | collective-permute-start | bytes 1572872 | tf_op jit(solution)/shard_map/ppermute | solution.py:27
  138.7 29.7 %collective-permute-start.2 = (bf16[256,1024]{1,0:T(8,128)(2,1)}, bf16[256,1024]{1,0:T(8,128)(2,1)}, u32[]{:S(2)}, u32[]{:S(2)}) collective-permute-start(bf16[256,1024]{1,0:T(8,128)(2,1)} %collective-permute-done), channel_id=1, source_target_pairs={{0,4},{4,8},{8,12},{12,0},{1,5},{5,9},{9,13},{13,1},{2,6},{6,10},{... | collective-permute-start | bytes 1572872 | tf_op jit(solution)/shard_map/ppermute | solution.py:22
  140.3 30.0 %copy-start.18 = (f32[1024]{0:T(1024)S(1)}, f32[1024]{0:T(1024)}, u32[]{:S(2)}) copy-start(f32[1024]{0:T(1024)} %param.26) | copy-start | bytes 12292
  174.9 23.2 %copy-start.19 = (bf16[512,1024]{1,0:T(8,128)(2,1)}, bf16[512,1024]{1,0:T(8,128)(2,1)S(1)}, u32[]{:S(2)}) copy-start(bf16[512,1024]{1,0:T(8,128)(2,1)S(1)} %get-tuple-element.126) | copy-start | bytes 3145732
  198.1 30.1 %copy-start.16 = (f32[256]{0:T(256)S(1)}, f32[256]{0:T(256)}, u32[]{:S(2)}) copy-start(f32[256]{0:T(256)} %param.28) | copy-start | bytes 3076
  198.1 43.1 %copy-start.5 = (bf16[512,256]{1,0:T(8,128)(2,1)S(1)}, bf16[512,256]{1,0:T(8,128)(2,1)}, u32[]{:S(2)}) copy-start(bf16[512,256]{1,0:T(8,128)(2,1)} %param.31) | copy-start | bytes 786436
  198.1 43.1 %copy-start.14 = (f32[256]{0:T(256)S(1)}, f32[256]{0:T(256)}, u32[]{:S(2)}) copy-start(f32[256]{0:T(256)} %param.29) | copy-start | bytes 3076
  198.1 49.8 %copy-start.17 = (f32[256]{0:T(256)S(1)}, f32[256]{0:T(256)}, u32[]{:S(2)}) copy-start(f32[256]{0:T(256)} %param.30) | copy-start | bytes 3076
  198.2 70.2 %all-gather.15.cloned.1.call-start = ((), (), s32[]{:S(2)}) async-start(), calls=%async_computation.14 | async-start | bytes 1310720 | tf_op jit(solution)/shard_map/all_gather | solution.py:60
  250.7 58.7 %reduce-scatter.13.cloned.1.call-start = ((), (), s32[]{:S(2)}) async-start(), calls=%async_computation.15 | async-start | bytes 2621440 | tf_op jit(solution)/shard_map/reduce_scatter | solution.py:68
  278.1 57.2 %all-gather.17.cloned.1.call-start = ((), (), s32[]{:S(2)}) async-start(), calls=%async_computation.16 | async-start | bytes 1310720 | tf_op jit(solution)/shard_map/all_gather | solution.py:60
  317.7 63.4 %reduce-scatter.23.cloned.1.call-start = ((), (), s32[]{:S(2)}) async-start(), calls=%async_computation.21 | async-start | bytes 2621440 | tf_op jit(solution)/shard_map/reduce_scatter | solution.py:204
  322.0 104.2 %reduce-scatter.21.cloned.1.call-start = ((), (), s32[]{:S(2)}) async-start(), calls=%async_computation.20 | async-start | bytes 2621440 | tf_op jit(solution)/shard_map/reduce_scatter | solution.py:201
  326.2 123.8 %reduce-scatter.19.cloned.1.call-start = ((), (), s32[]{:S(2)}) async-start(), calls=%async_computation.19 | async-start | bytes 655360 | tf_op jit(solution)/shard_map/reduce_scatter | solution.py:198
  337.0 6.0 %copy-start.1 = (bf16[512,1024]{1,0:T(8,128)(2,1)S(1)}, bf16[512,1024]{1,0:T(8,128)(2,1)}, u32[]{:S(2)}) copy-start(bf16[512,1024]{1,0:T(8,128)(2,1)} %all-gather.17.cloned.1.call-done) | copy-start | bytes 3145732
  344.3 141.8 %reduce-scatter.17.cloned.1.call-start = ((), (), s32[]{:S(2)}) async-start(), calls=%async_computation.18 | async-start | bytes 1966080 | tf_op jit(solution)/shard_map/reduce_scatter | solution.py:195
  356.4 7.7 %copy-start.10 = (bf16[512,1,256]{2,0,1:T(8,128)(2,1)S(1)}, bf16[512,1,256]{2,0,1:T(8,128)(2,1)}, u32[]{:S(2)}) copy-start(bf16[512,1,256]{2,0,1:T(8,128)(2,1)} %copy.38) | copy-start | bytes 786436
  367.5 154.0 %reduce-scatter.15.cloned.1.call-start = ((), (), s32[]{:S(2)}) async-start(), calls=%async_computation.17 | async-start | bytes 2621440 | tf_op jit(solution)/shard_map/reduce_scatter | solution.py:68
  371.3 201.1 %all-reduce.6.cloned.1.call-start = ((), (), s32[]{:S(2)}) async-start(), calls=%async_computation.22 | async-start | bytes 3145728 | tf_op jit(solution)/shard_map/psum | solution.py:209
  (7 other events, 20.8 us)
Sparse Core Ops, SparseCore 0:
  9.5 19.5 all-gather.6
  31.3 37.6 all-gather.8
  78.0 29.3 reduce-scatter.8
  121.3 17.6 all-gather.10
  140.4 53.5 all-gather.12
  198.3 29.8 reduce-scatter.10
  250.8 17.5 all-gather.14
  278.2 31.1 reduce-scatter.12
  317.8 17.4 all-gather.16
  337.4 43.6 reduce-scatter.22
  383.4 42.8 reduce-scatter.20
  429.0 21.0 reduce-scatter.18
  452.3 33.6 reduce-scatter.16
  488.5 29.9 reduce-scatter.14
  520.8 51.5 all-reduce.5
